TPU v7x, 32 devices: a whole 2x2x4 slice. The times are simulated.
32 devices in a mesh: head: 4 (over y, x), batch: 8 (over z, core).
Axes of the slice: x: 2, y: 2, z: 4, core: 2. Of those that a mesh axis runs over, the one named last changes fastest.
Arguments:
- hidden_in: bfloat16 [8, 256, 4096], P('batch', None, 'head')
- w_query: bfloat16 [4096, 4096], P('batch', 'head'), may hold values from -0.09375 to 0.09375
- w_key: bfloat16 [4096, 4096], P('batch', 'head'), may hold values from -0.09375 to 0.09375
- w_value: bfloat16 [4096, 4096], P('batch', 'head'), may hold values from -0.09375 to 0.09375
- w_beta: bfloat16 [4096, 32], P('batch', 'head'), may hold values from -0.09375 to 0.09375
- w_out: bfloat16 [4096, 4096], P('head', 'batch'), may hold values from -0.125 to 0.125
- mem_pos: int32 [8, 2, 64], P('batch'), may hold values from 0 to 127, as said below
- memory_in: float32 [8, 32, 128, 128], P('batch', 'head'), may hold values from -6 to 6
Outputs:
- hidden_out: bfloat16 [8, 256, 4096], P('batch', None, 'head')
- memory_out: float32 [8, 32, 128, 128], P('batch', 'head')
Inputs may be any that keep to these rules, and one draw needn't show every extreme that they name: `mem_pos`: within each sequence and segment the 64 positions are distinct and ascending.
All inputs are finite; a program needn't handle non-finite values.
Results may differ from a plain program's by a relative error of at most 0.005.
Values may be sent and summed in bfloat16 or wider, within the bound.
No kernel may reach another device: no remote copies, remote signals or barrier semaphores. Data moves between devices by JAX's collectives and lax.ppermute only.
A program may use at most 128 MiB of HBM per device.

v0:
```python
import jax
import jax.numpy as jnp
from jax import lax
from jax.sharding import PartitionSpec as P

SEGS = 2
epsilon = 1e-05


def recur(query, keys, values, beta, state):
    highest = lax.Precision.HIGHEST
    readouts = []
    for segment in range(query.shape[1]):
        readouts.append(
            jnp.einsum("bhij,blhj->blhi", state, query[:, segment], precision=highest).astype(
                jnp.bfloat16
            )
        )
        recalled = jnp.einsum("bhij,bmhj->bmhi", state, keys[:, segment], precision=highest)
        change = beta[:, segment][..., None] * (values[:, segment] - recalled)
        state = state + jnp.einsum("bmhi,bmhj->bhij", change, keys[:, segment], precision=highest)
    return (jnp.stack(readouts, axis=1), state)


def body(hidden_in, w_query, w_key, w_value, w_beta, w_out, mem_pos, memory_in):
    seq_count, row_count, local_width = hidden_in.shape
    seg_rows = row_count // SEGS
    mem_count = mem_pos.shape[2]
    local_heads = w_beta.shape[1]
    local_features = w_query.shape[1]
    head_size = local_features // local_heads
    x_float = hidden_in.astype(jnp.float32)
    whole = lax.all_gather(hidden_in, "head", axis=2, tiled=True)
    whole_float = whole.astype(jnp.float32)
    mean_square = jnp.mean(whole_float * whole_float, axis=2, keepdims=True)
    normed = (whole_float * lax.rsqrt(mean_square + epsilon)).astype(jnp.bfloat16)
    full_width = normed.shape[2]
    offsets = (jnp.arange(SEGS, dtype=jnp.int32) * seg_rows)[None, :, None]
    picked = (mem_pos + offsets).reshape(seq_count, SEGS * mem_count)
    memory_rows = jax.vmap(lambda block, where: jnp.take(block, where, axis=0))(normed, picked)
    memory_rows = memory_rows.reshape(seq_count * SEGS * mem_count, full_width)
    token_rows = normed.reshape(seq_count * row_count, full_width)
    piece_query = lax.all_gather(w_query, "batch", axis=0, tiled=True)
    piece_key = lax.all_gather(w_key, "batch", axis=0, tiled=True)
    piece_value = lax.all_gather(w_value, "batch", axis=0, tiled=True)
    piece_beta = lax.all_gather(w_beta, "batch", axis=0, tiled=True)
    query = jnp.dot(token_rows, piece_query, preferred_element_type=jnp.float32)
    keys = jnp.dot(memory_rows, piece_key, preferred_element_type=jnp.float32)
    values = jnp.dot(memory_rows, piece_value, preferred_element_type=jnp.float32)
    logits = jnp.dot(memory_rows, piece_beta, preferred_element_type=jnp.float32)
    query = (query * head_size ** (-0.5)).reshape(seq_count, SEGS, seg_rows, local_heads, head_size)
    keys = keys.reshape(seq_count, SEGS, mem_count, local_heads, head_size)
    keys = keys * lax.rsqrt(jnp.sum(keys * keys, axis=-1, keepdims=True) + 1e-06)
    values = values.reshape(seq_count, SEGS, mem_count, local_heads, head_size)
    beta = jax.nn.sigmoid(logits).reshape(seq_count, SEGS, mem_count, local_heads)
    readout, state = recur(query, keys, values, beta, memory_in)
    readout = readout.reshape(seq_count * row_count, local_features)
    terms = jnp.dot(
        readout,
        lax.all_gather(w_out, "batch", axis=1, tiled=True),
        preferred_element_type=jnp.float32,
    )
    mixed = lax.psum_scatter(terms, "head", scatter_dimension=1, tiled=True)
    hidden_out = (mixed + x_float.reshape(seq_count * row_count, local_width)).astype(jnp.bfloat16)
    return (hidden_out.reshape(hidden_in.shape), state)


def solution(mesh):
    in_specs = (
        P("batch", None, "head"),
        P("batch", "head"),
        P("batch", "head"),
        P("batch", "head"),
        P("batch", "head"),
        P("head", "batch"),
        P("batch", None, None),
        P("batch", "head", None, None),
    )
    out_specs = (P("batch", None, "head"), P("batch", "head", None, None))
    return jax.shard_map(body, mesh=mesh, in_specs=in_specs, out_specs=out_specs, check_vma=False)
```

profile of v0, /device:TPU:0, one launch (start us, length us, event | category | flops | bytes accessed | tf_op | source)
XLA Modules:
  0.0 445.6 jit_solution(10736198151364103323)
XLA Ops:
  10.6 0.8 broadcast_add_fusion
  11.5 15.9 %all_gather.20 = bf16[4096,8]{0,1:T(8,128)(2,1)S(1)} all-gather(bf16[512,8]{0,1:T(8,128)(2,1)} %param.12), channel_id=1, replica_groups=mesh['head'=4,'batch'=8] {'batch'}, dimensions={0}, use_global_device_ids=true | all-gather | bytes 73728 | tf_op jit(solution)/shard_map/all_gather | solution.py:46
  27.4 20.3 %all-gather.6.cloned.1.call-done = bf16[1,256,4096]{2,1,0:T(8,128)(2,1)} async-done(((bf16[1,256,1024]{2,1,0:T(8,128)(2,1)}), bf16[1,256,4096]{2,1,0:T(8,128)(2,1)}) %all-gather.6.cloned.1.call-update) | async-done | bytes 2097168 | tf_op jit(solution)/shard_map/all_gather | solution.py:33
  47.8 2.1 fusion
  49.8 2.2 fusion.1
  52.0 3.7 gather_fusion
  56.3 1.2 bitcast_select_fusion
  57.5 73.9 %all-gather.12.cloned.1.call-done = bf16[4096,1024]{1,0:T(8,128)(2,1)} async-done(((bf16[512,1024]{1,0:T(8,128)(2,1)}), bf16[4096,1024]{1,0:T(8,128)(2,1)}) %all-gather.12.cloned.1.call-update) | async-done | bytes 8388624 | tf_op jit(solution)/shard_map/all_gather | solution.py:44
  131.4 4.7 %convolution_bitcast_fusion.2 = f32[16,8,8,128]{3,1,2,0:T(8,128)S(1)} fusion(bf16[4096,1024]{1,0:T(8,128)(2,1)} %all-gather.12.cloned.1.call-done, bf16[128,4096]{1,0:T(8,128)(2,1)S(1)} %gather_fusion, pred[128]{0:T(512)(128)(4,1)S(1)} %compare_and_fusion), kind=kOutput, calls=%fused_computation.11 | convolution fusion | flops 1074266112 | bytes 9961600 | tf_op jit(solution)/shard_map/dot_general | solution.py:48
  136.5 77.1 %all-gather.10.cloned.1.call-done = bf16[4096,1024]{1,0:T(8,128)(2,1)} async-done(((bf16[512,1024]{1,0:T(8,128)(2,1)}), bf16[4096,1024]{1,0:T(8,128)(2,1)}) %all-gather.10.cloned.1.call-update) | async-done | bytes 8388624 | tf_op jit(solution)/shard_map/all_gather | solution.py:45
  213.6 12.1 %copy.27 = bf16[1024,4096]{1,0:T(8,128)(2,1)} copy(bf16[1024,4096]{0,1:T(8,128)(2,1)} %bitcast.131) | data formatting | bytes 16777216 | tf_op jit(solution)/shard_map/dot_general | solution.py:49
  225.7 69.9 %all-gather.8.cloned.1.call-done = bf16[4096,1024]{1,0:T(8,128)(2,1)} async-done(((bf16[512,1024]{1,0:T(8,128)(2,1)}), bf16[4096,1024]{1,0:T(8,128)(2,1)}) %all-gather.8.cloned.1.call-update) | async-done | bytes 8388624 | tf_op jit(solution)/shard_map/all_gather | solution.py:43
  295.6 5.9 %fusion.7 = f32[32,8,8,128]{3,1,2,0:T(8,128)S(1)} fusion(bf16[4096,1024]{1,0:T(8,128)(2,1)} %all-gather.8.cloned.1.call-done, bf16[1,256,4096]{2,1,0:T(8,128)(2,1)S(1)} %fusion.1), kind=kOutput, calls=%fused_computation.8 | convolution fusion | flops 2147745792 | bytes 11534336 | tf_op jit(solution)/shard_map/dot_general | solution.py:47
  301.7 1.2 fusion.12
  303.2 2.9 convolution_bitcast_fusion.3
  306.1 1.1 fusion.17
  307.2 1.0 fusion.10
  308.3 1.2 fusion.13
  309.9 67.7 %all-gather.14.cloned.1.call-done = bf16[1024,4096]{1,0:T(8,128)(2,1)} async-done(((bf16[1024,512]{1,0:T(8,128)(2,1)}), bf16[1024,4096]{1,0:T(8,128)(2,1)}) %all-gather.14.cloned.1.call-update) | async-done | bytes 8388624 | tf_op jit(solution)/shard_map/all_gather | solution.py:60
  377.6 7.7 %fusion.25 = f32[256,4096]{1,0:T(8,128)} fusion(bf16[1024,4096]{1,0:T(8,128)(2,1)} %all-gather.14.cloned.1.call-done, bf16[32,8,8,128]{3,2,1,0:T(8,128)(2,1)S(1)} %bitcast.136), kind=kOutput, calls=%fused_computation.36 | convolution fusion | flops 2147483648 | bytes 13107200 | tf_op jit(solution)/shard_map/dot_general | solution.py:58
  385.4 1.1 fusion.19
  386.5 1.8 fusion.11
  388.3 48.3 %reduce-scatter.2.cloned.1.call-done = f32[256,1024]{1,0:T(8,128)} async-done(((f32[256,4096]{1,0:T(8,128)}), f32[256,1024]{1,0:T(8,128)}) %reduce-scatter.2.cloned.1.call-update) | async-done | bytes 1048592 | tf_op jit(solution)/shard_map/reduce_scatter | solution.py:63
  436.6 2.2 fusion.24
  (40 shorter events, 5.4 us)
Async XLA Ops:
  7.2 40.6 %all-gather.6.cloned.1.call-start = ((), (), s32[]{:S(2)}) async-start(), calls=%async_computation.1 | async-start | bytes 2621440 | tf_op jit(solution)/shard_map/all_gather | solution.py:33
  7.9 123.5 %all-gather.12.cloned.1.call-start = ((), (), s32[]{:S(2)}) async-start(), calls=%async_computation.4 | async-start | bytes 9437184 | tf_op jit(solution)/shard_map/all_gather | solution.py:44
  8.6 204.9 %all-gather.10.cloned.1.call-start = ((), (), s32[]{:S(2)}) async-start(), calls=%async_computation.3 | async-start | bytes 9437184 | tf_op jit(solution)/shard_map/all_gather | solution.py:45
  9.4 286.2 %all-gather.8.cloned.1.call-start = ((), (), s32[]{:S(2)}) async-start(), calls=%async_computation.2 | async-start | bytes 9437184 | tf_op jit(solution)/shard_map/all_gather | solution.py:43
  10.0 367.6 %all-gather.14.cloned.1.call-start = ((), (), s32[]{:S(2)}) async-start(), calls=%async_computation.5 | async-start | bytes 9437184 | tf_op jit(solution)/shard_map/all_gather | solution.py:60
  10.5 426.0 %reduce-scatter.2.cloned.1.call-start = ((), (), s32[]{:S(2)}) async-start(), calls=%async_computation.6 | async-start | bytes 5242880 | tf_op jit(solution)/shard_map/reduce_scatter | solution.py:63
  225.7 76.1 %copy-start.1 = (f32[1,8,128,128]{3,2,1,0:T(8,128)S(1)}, f32[1,8,128,128]{3,2,1,0:T(8,128)}, u32[]{:S(2)}) copy-start(f32[1,8,128,128]{3,2,1,0:T(8,128)} %param.15) | copy-start | bytes 1572868
  295.6 7.6 %copy-start = (bf16[1024,4096]{1,0:T(8,128)(2,1)S(1)}, bf16[1024,4096]{1,0:T(8,128)(2,1)}, u32[]{:S(2)}) copy-start(bf16[1024,4096]{1,0:T(8,128)(2,1)} %copy.27) | copy-start | bytes 25165828
  295.6 7.6 %copy-start.2 = (bf16[1,128,1,1,1,1,4096]{6,1,5,4,3,2,0:T(8,128)(2,1)S(1)}, bf16[1,128,1,1,1,1,4096]{6,1,5,4,3,2,0:T(8,128)(2,1)}, u32[]{:S(2)}) copy-start(bf16[1,128,1,1,1,1,4096]{6,1,5,4,3,2,0:T(8,128)(2,1)} %bitcast_select_fusion) | copy-start | bytes 3145732
  377.6 59.0 %copy-start.3 = (bf16[1,256,1024]{2,1,0:T(8,128)(2,1)S(1)}, bf16[1,256,1024]{2,1,0:T(8,128)(2,1)}, u32[]{:S(2)}) copy-start(bf16[1,256,1024]{2,1,0:T(8,128)(2,1)} %param.8) | copy-start | bytes 1572868
Sparse Core Ops, SparseCore 0:
  9.8 37.8 all-gather.5
  49.3 82.0 all-gather.11
  133.0 80.5 all-gather.9
  215.0 80.5 all-gather.7
  297.0 80.5 all-gather.13
  385.5 51.0 reduce-scatter.1
where the time goes:
time: 446 us
  waiting for transfers between devices  360 us (81%)
  matrix products  29.1 us (7%)
  local copies, waits for them, and re-layouts  16.9 us (4%)
  blocking collectives  15.9 us (4%)
  between operations  14.3 us (3%)
  other arithmetic  8.83 us (2%)
    all_gather x1, waiting for transfers between devices, body(): piece_value = lax.all_gather(w_value, 'batch', axis=0, tiled=True)  77.1 us
    all_gather x1, waiting for transfers between devices, body(): piece_key = lax.all_gather(w_key, 'batch', axis=0, tiled=True)  73.9 us
    all_gather x1, waiting for transfers between devices, body(): piece_query = lax.all_gather(w_query, 'batch', axis=0, tiled=True)  69.9 us
    all_gather x1, waiting for transfers between devices, body(): lax.all_gather(w_out, 'batch', axis=1, tiled=True)  67.7 us
    reduce_scatter x1, waiting for transfers between devices, body(): mixed = lax.psum_scatter(terms, 'head', scatter_dimension=1, tiled=True)  48.3 us
    all_gather x1, waiting for transfers between devices, body(): whole = lax.all_gather(hidden_in, 'head', axis=2, tiled=True)  20.3 us
    all_gather x1, blocking collectives, body(): piece_beta = lax.all_gather(w_beta, 'batch', axis=0, tiled=True)  15.9 us
    dot_general x1, local copies, waits for them, and re-layouts, body(): jnp.dot(memory_rows, piece_value, preferred_element_type=jnp.float32)  12.1 us
  transfers between devices with their start and end apart: 6, of which 6 were waited for; matrix products, arithmetic and copies ran while one was open for 10% of the time, Pallas kernels for 0%

commit v1 on v0

--- a/solution.py
+++ b/solution.py
@@ -41,7 +41,15 @@
     memory_rows = memory_rows.reshape(seq_count * SEGS * mem_count, full_width)
     token_rows = normed.reshape(seq_count * row_count, full_width)
     piece_query = lax.all_gather(w_query, "batch", axis=0, tiled=True)
-    piece_key = lax.all_gather(w_key, "batch", axis=0, tiled=True)
+    ways, here, step = (lax.axis_size("batch"), lax.axis_index("batch"), w_key.shape[0])
+    line, have = (w_key, 1)
+    while have < ways:
+        line = jnp.concatenate(
+            [line, lax.ppermute(line, "batch", [(d, (d - have) % ways) for d in range(ways)])],
+            axis=0,
+        )
+        have = 2 * have
+    piece_key = jnp.roll(line, here * step, axis=0)
     piece_value = lax.all_gather(w_value, "batch", axis=0, tiled=True)
     piece_beta = lax.all_gather(w_beta, "batch", axis=0, tiled=True)
     query = jnp.dot(token_rows, piece_query, preferred_element_type=jnp.float32)

time: 446 us -> 566 us (1.27)
  blocking collectives: 15.9 us -> 321 us
  waiting for transfers between devices: 360 us -> 145 us
  local copies, waits for them, and re-layouts: 16.9 us -> 35.2 us
    all_gather x1, blocking collectives: 15.9 us -> 321 us  [body(): piece_beta = lax.all_gather(w_beta, 'batch', axis=0, tiled=True)]
    ppermute x0 -> x3, waiting for transfers between devices: none -> 94 us  [body(): lax.ppermute(line, 'batch', [(d, (d - have) % ways) for d in range(ways)])]
    all_gather x1, waiting for transfers between devices: 77.1 us -> 0.02 us  [body(): piece_value = lax.all_gather(w_value, 'batch', axis=0, tiled=True)]
    all_gather x1 -> x0, waiting for transfers between devices: 73.9 us -> none  [body(): piece_key = lax.all_gather(w_key, 'batch', axis=0, tiled=True)]
    all_gather x1, waiting for transfers between devices: 69.9 us -> 0.01 us  [body(): piece_query = lax.all_gather(w_query, 'batch', axis=0, tiled=True)]
    all_gather x1, waiting for transfers between devices: 67.7 us -> 0.02 us  [body(): lax.all_gather(w_out, 'batch', axis=1, tiled=True)]
    all_gather x1, waiting for transfers between devices: 20.3 us -> 0.01 us  [body(): whole = lax.all_gather(hidden_in, 'head', axis=2, tiled=True)]
    unnamed x10 -> x37, local copies, waits for them, and re-layouts: 0.31 us -> 13.5 us
  transfers between devices with their start and end apart: 6 -> 8, of which waited for: 6 -> 3; matrix products, arithmetic and copies ran while one was open for 10% -> 12% of each run, Pallas kernels for 0% -> 0%
where the time goes in v1:
time: 566 us; the launch traced here: 565 us
  blocking collectives  321 us (57%)
  waiting for transfers between devices  145 us (26%)
  local copies, waits for them, and re-layouts  35.2 us (6%)
  matrix products  31.4 us (6%)
  between operations  14 us (2%)
  other arithmetic  13.9 us (2%)
    all_gather x1, blocking collectives, body(): piece_beta = lax.all_gather(w_beta, 'batch', axis=0, tiled=True)  321 us
    ppermute x3, waiting for transfers between devices, body(): lax.ppermute(line, 'batch', [(d, (d - have) % ways) for d in range(ways)])  94 us
    reduce_scatter x1, waiting for transfers between devices, body(): mixed = lax.psum_scatter(terms, 'head', scatter_dimension=1, tiled=True)  48 us
    unnamed x37, local copies, waits for them, and re-layouts  13.5 us
    dot_general x1, local copies, waits for them, and re-layouts, body(): jnp.dot(memory_rows, piece_value, preferred_element_type=jnp.float32)  11.5 us
  transfers between devices with their start and end apart: 8, of which 3 were waited for; matrix products, arithmetic and copies ran while one was open for 12% of the time, Pallas kernels for 0%

profile of v1, /device:TPU:0, one launch (start us, length us, event | category | flops | bytes accessed | tf_op | source)
XLA Modules:
  0.0 565.0 jit_solution(6564479289817047539)
XLA Ops:
  10.0 4.6 collective-permute-start
  14.6 12.6 %collective-permute-done = bf16[512,1024]{1,0:T(8,128)(2,1)S(1)} collective-permute-done((bf16[512,1024]{1,0:T(8,128)(2,1)}, bf16[512,1024]{1,0:T(8,128)(2,1)S(1)}, u32[]{:S(2)}, u32[]{:S(2)}) %collective-permute-start) | collective-permute-done | bytes 1048608 | tf_op jit(solution)/shard_map/ppermute | solution.py:48
  27.2 1.9 pad_maximum_fusion.1
  29.7 81.4 %collective-permute-done.1 = bf16[1024,1024]{1,0:T(8,128)(2,1)S(1)} collective-permute-done((bf16[1024,1024]{1,0:T(8,128)(2,1)S(1)}, bf16[1024,1024]{1,0:T(8,128)(2,1)S(1)}, u32[]{:S(2)}, u32[]{:S(2)}) %collective-permute-start.1) | collective-permute-done | bytes 2097184 | tf_op jit(solution)/shard_map/ppermute | solution.py:48
  111.1 2.5 pad_maximum_fusion
  113.8 320.6 %all_gather.17 = bf16[4096,8]{0,1:T(8,128)(2,1)S(1)} all-gather(bf16[512,8]{0,1:T(8,128)(2,1)S(1)} %copy-done.12), channel_id=1, replica_groups=mesh['head'=4,'batch'=8] {'batch'}, dimensions={0}, use_global_device_ids=true | all-gather | bytes 73728 | tf_op jit(solution)/shard_map/all_gather | solution.py:54
  435.5 2.3 constant_dynamic-update-slice_fusion.6
  439.3 2.1 fusion.2
  441.4 2.2 fusion.3
  443.6 4.8 gather_fusion
  448.4 1.7 fusion.27
  450.1 2.5 bitcast_select_fusion
  452.7 4.6 constant_dynamic-update-slice_fusion.4
  459.5 1.5 constant_dynamic-update-slice_fusion.1
  461.0 4.6 constant_dynamic-update-slice_fusion
  465.6 4.7 fusion.12
  471.0 11.5 %copy.27 = bf16[1024,4096]{1,0:T(8,128)(2,1)} copy(bf16[1024,4096]{0,1:T(8,128)(2,1)} %bitcast.130) | data formatting | bytes 16777216 | tf_op jit(solution)/shard_map/dot_general | solution.py:57
  482.5 5.9 %fusion.9 = f32[32,8,8,128]{3,1,2,0:T(8,128)S(1)} fusion(bf16[4096,1024]{1,0:T(8,128)(2,1)} %all-gather.7.cloned.1.call-done, bf16[1,256,4096]{2,1,0:T(8,128)(2,1)S(1)} %fusion.3), kind=kOutput, calls=%fused_computation.12 | convolution fusion | flops 2147745792 | bytes 11534336 | tf_op jit(solution)/shard_map/dot_general | solution.py:55
  489.9 2.9 convolution_bitcast_fusion.2
  494.0 2.0 fusion.15
  497.6 7.7 %fusion.30 = f32[256,4096]{1,0:T(8,128)} fusion(bf16[1024,4096]{1,0:T(8,128)(2,1)} %all-gather.11.cloned.1.call-done, bf16[32,8,8,128]{3,2,1,0:T(8,128)(2,1)S(1)} %bitcast.135), kind=kOutput, calls=%fused_computation.40 | convolution fusion | flops 2147483648 | bytes 13107200 | tf_op jit(solution)/shard_map/dot_general | solution.py:66
  506.6 1.8 fusion.16
  508.4 48.0 %reduce-scatter.2.cloned.1.call-done = f32[256,1024]{1,0:T(8,128)} async-done(((f32[256,4096]{1,0:T(8,128)}), f32[256,1024]{1,0:T(8,128)}) %reduce-scatter.2.cloned.1.call-update) | async-done | bytes 1048592 | tf_op jit(solution)/shard_map/reduce_scatter | solution.py:71
  556.3 2.2 fusion.29
  (73 shorter events, 14.6 us)
Async XLA Ops:
  7.2 104.0 %copy-start.3 = (bf16[512,1024]{1,0:T(8,128)(2,1)S(1)}, bf16[512,1024]{1,0:T(8,128)(2,1)}, u32[]{:S(2)}) copy-start(bf16[512,1024]{1,0:T(8,128)(2,1)} %param.10) | copy-start | bytes 3145732
  7.2 106.4 %copy-start.13 = (s32[1,2,64]{2,1,0:T(2,128)S(1)}, s32[1,2,64]{2,1,0:T(2,128)}, u32[]{:S(2)}) copy-start(s32[1,2,64]{2,1,0:T(2,128)} %param.14) | copy-start | bytes 1540
  7.2 106.6 %copy-start.12 = (bf16[512,8]{0,1:T(8,128)(2,1)S(1)}, bf16[512,8]{0,1:T(8,128)(2,1)}, u32[]{:S(2)}) copy-start(bf16[512,8]{0,1:T(8,128)(2,1)} %param.12) | copy-start | bytes 24580
  7.2 432.1 %all-gather.5.cloned.1.call-start = ((), (), s32[]{:S(2)}) async-start(), calls=%async_computation.1 | async-start | bytes 2621440 | tf_op jit(solution)/shard_map/all_gather | solution.py:33
  7.9 463.0 %all-gather.9.cloned.1.call-start = ((), (), s32[]{:S(2)}) async-start(), calls=%async_computation.3 | async-start | bytes 9437184 | tf_op jit(solution)/shard_map/all_gather | solution.py:53
  8.7 473.8 %all-gather.7.cloned.1.call-start = ((), (), s32[]{:S(2)}) async-start(), calls=%async_computation.2 | async-start | bytes 9437184 | tf_op jit(solution)/shard_map/all_gather | solution.py:43
  9.4 488.2 %all-gather.11.cloned.1.call-start = ((), (), s32[]{:S(2)}) async-start(), calls=%async_computation.4 | async-start | bytes 9437184 | tf_op jit(solution)/shard_map/all_gather | solution.py:68
  10.0 546.3 %reduce-scatter.2.cloned.1.call-start = ((), (), s32[]{:S(2)}) async-start(), calls=%async_computation.5 | async-start | bytes 5242880 | tf_op jit(solution)/shard_map/reduce_scatter | solution.py:71
  10.0 17.2 %collective-permute-start = (bf16[512,1024]{1,0:T(8,128)(2,1)}, bf16[512,1024]{1,0:T(8,128)(2,1)S(1)}, u32[]{:S(2)}, u32[]{:S(2)}) collective-permute-start(bf16[512,1024]{1,0:T(8,128)(2,1)} %param.10), channel_id=1, source_target_pairs={{0,7},{1,0},{2,1},{3,2},{4,3},{5,4},{6,5},{7,6},{8,15},{9,8},{10,9... | collective-permute-start | bytes 3145736 | tf_op jit(solution)/shard_map/ppermute | solution.py:48
  27.2 83.9 %copy-start.4 = (bf16[512,1024]{1,0:T(8,128)(2,1)}, bf16[512,1024]{1,0:T(8,128)(2,1)S(1)}, u32[]{:S(2)}) copy-start(bf16[512,1024]{1,0:T(8,128)(2,1)S(1)} %collective-permute-done) | copy-start | bytes 3145732
  29.1 82.0 %collective-permute-start.1 = (bf16[1024,1024]{1,0:T(8,128)(2,1)S(1)}, bf16[1024,1024]{1,0:T(8,128)(2,1)S(1)}, u32[]{:S(2)}, u32[]{:S(2)}) collective-permute-start(bf16[1024,1024]{1,0:T(8,128)(2,1)S(1)} %pad_maximum_fusion.1), channel_id=1, source_target_pairs={{0,6},{1,7},{2,0},{3,1},{4,2},{5,3},{6,4},{7,5},{8,14},{9,15},{10,... | collective-permute-start | bytes 6291464 | tf_op jit(solution)/shard_map/ppermute | solution.py:48
  111.1 328.2 %copy-start.1 = (bf16[1024,1024]{1,0:T(8,128)(2,1)}, bf16[1024,1024]{1,0:T(8,128)(2,1)S(1)}, u32[]{:S(2)}) copy-start(bf16[1024,1024]{1,0:T(8,128)(2,1)S(1)} %collective-permute-done.1) | copy-start | bytes 6291460
  113.6 339.1 %collective-permute-start.2 = (bf16[2048,1024]{1,0:T(8,128)(2,1)}, bf16[2048,1024]{1,0:T(8,128)(2,1)}, u32[]{:S(2)}, u32[]{:S(2)}) collective-permute-start(bf16[2048,1024]{1,0:T(8,128)(2,1)} %pad_maximum_fusion), channel_id=1, source_target_pairs={{0,4},{1,5},{2,6},{3,7},{4,0},{5,1},{6,2},{7,3},{8,12},{9,13},{10,... | collective-permute-start | bytes 12582920 | tf_op jit(solution)/shard_map/ppermute | solution.py:48
  450.1 8.4 %copy-start.5 = (bf16[512,1024]{1,0:T(8,128)(2,1)S(1)}, bf16[512,1024]{1,0:T(8,128)(2,1)}, u32[]{:S(2)}) copy-start(bf16[512,1024]{1,0:T(8,128)(2,1)} %copy-done.4) | copy-start | bytes 3145732
  450.1 9.4 %copy-start.2 = (bf16[1024,1024]{1,0:T(8,128)(2,1)S(1)}, bf16[1024,1024]{1,0:T(8,128)(2,1)}, u32[]{:S(2)}) copy-start(bf16[1024,1024]{1,0:T(8,128)(2,1)} %copy-done.1) | copy-start | bytes 6291460
  457.3 8.3 %copy-start.6 = (bf16[128,4096]{1,0:T(8,128)(2,1)S(1)}, bf16[128,4096]{1,0:T(8,128)(2,1)}, u32[]{:S(2)}) copy-start(bf16[128,4096]{1,0:T(8,128)(2,1)} %gather_fusion) | copy-start | bytes 3145732
  470.9 21.9 %copy-start.8 = (f32[1,2,64,8,128]{4,2,3,1,0:T(8,128)}, f32[1,2,64,8,128]{4,2,3,1,0:T(8,128)S(1)}, u32[]{:S(2)}) copy-start(f32[1,2,64,8,128]{4,2,3,1,0:T(8,128)S(1)} %copy_multiply_fusion) | copy-start | bytes 1572868
  482.5 6.2 %copy-start.7 = (f32[1,8,128,128]{3,2,1,0:T(8,128)S(1)}, f32[1,8,128,128]{3,2,1,0:T(8,128)}, u32[]{:S(2)}) copy-start(f32[1,8,128,128]{3,2,1,0:T(8,128)} %param.15) | copy-start | bytes 1572868
  482.5 7.4 %copy-start = (bf16[1024,4096]{1,0:T(8,128)(2,1)S(1)}, bf16[1024,4096]{1,0:T(8,128)(2,1)}, u32[]{:S(2)}) copy-start(bf16[1024,4096]{1,0:T(8,128)(2,1)} %copy.27) | copy-start | bytes 25165828
  482.5 7.4 %copy-start.10 = (bf16[1,128,1,1,1,1,4096]{6,1,5,4,3,2,0:T(8,128)(2,1)S(1)}, bf16[1,128,1,1,1,1,4096]{6,1,5,4,3,2,0:T(8,128)(2,1)}, u32[]{:S(2)}) copy-start(bf16[1,128,1,1,1,1,4096]{6,1,5,4,3,2,0:T(8,128)(2,1)} %bitcast_select_fusion) | copy-start | bytes 3145732
  497.6 7.8 %copy-start.9 = (f32[1,2,64,8,128]{4,2,3,1,0:T(8,128)S(1)}, f32[1,2,64,8,128]{4,2,3,1,0:T(8,128)}, u32[]{:S(2)}) copy-start(f32[1,2,64,8,128]{4,2,3,1,0:T(8,128)} %copy-done.8) | copy-start | bytes 1572868
  497.6 58.7 %copy-start.11 = (bf16[1,256,1024]{2,1,0:T(8,128)(2,1)S(1)}, bf16[1,256,1024]{2,1,0:T(8,128)(2,1)}, u32[]{:S(2)}) copy-start(bf16[1,256,1024]{2,1,0:T(8,128)(2,1)} %param.8) | copy-start | bytes 1572868
Sparse Core Ops, SparseCore 0:
  9.8 37.8 all-gather.4
  49.4 202.2 all-gather.8
  253.3 119.5 all-gather.6
  374.4 86.4 all-gather.10
  505.5 50.7 reduce-scatter.1
